TPU v7x, 32 devices: a whole 2x2x4 slice. The times are simulated.
32 devices in a mesh: expert: 16 (over z, y, core), hidden: 2 (over x).
Axes of the slice: x: 2, y: 2, z: 4, core: 2. Of those that a mesh axis runs over, the one named last changes fastest.
Arguments:
- tokens: bfloat16 [2048, 4096], P('expert'), may hold values from -6 to 6
- enc_weight: bfloat16 [4096, 1024], P('expert', 'hidden'), may hold values from -0.09375 to 0.09375
- routes: int32 [2048, 8], P('expert'), may hold values from 0 to 15, all different within a row; in each aligned block of 128 rows (0 to 127, 128 to 255, ...) at most 128 rows name the same one
- gates: float32 [2048, 8], P('expert'), may hold values from 0.1 to 1
- gate_weight: bfloat16 [16, 1024, 1536], P('expert', None, 'hidden'), may hold values from -0.1875 to 0.1875
- up_weight: bfloat16 [16, 1024, 1536], P('expert', None, 'hidden'), may hold values from -0.1875 to 0.1875
- down_weight: bfloat16 [16, 1536, 1024], P('expert', None, 'hidden'), may hold values from -0.15625 to 0.15625
- dec_weight: bfloat16 [1024, 4096], P('expert', 'hidden'), may hold values from -0.1875 to 0.1875
Outputs:
- mixed: bfloat16 [2048, 4096], P('expert', 'hidden')
Inputs may be any that keep to these rules, and one draw needn't show every extreme that they name: `routes`: each row names 8 different experts; within one group of 128 consecutive tokens no expert is named more than 128 times.
All inputs are finite; a program needn't handle non-finite values.
Results may differ from a plain program's by a relative error of at most 0.0076.
Values may be sent and summed in bfloat16 or wider, within the bound.
A program may use at most 64 MiB of HBM per device.

v0:
```python
import jax
import jax.numpy as jnp
from jax import lax
from jax.sharding import PartitionSpec as P


def on_device(tokens, enc_weight, routes, gates, gate_weight, up_weight, down_weight, dec_weight):
    groups = lax.axis_size("expert")
    token_count, choice_count = routes.shape
    capacity = min(token_count, 2 * token_count * choice_count // groups)
    columns = tokens
    latent = jnp.dot(
        columns,
        lax.all_gather(enc_weight, "expert", axis=0, tiled=True),
        preferred_element_type=jnp.float32,
    ).astype(jnp.bfloat16)
    payload = lax.all_gather(latent, "hidden", axis=1, tiled=True)
    chosen = routes.reshape(-1)
    onehot = (chosen[:, None] == jnp.arange(groups, dtype=jnp.int32)[None, :]).astype(jnp.int32)
    position = jnp.sum((jnp.cumsum(onehot, axis=0) - onehot) * onehot, axis=1)
    target = chosen * capacity + position
    source_row = jnp.arange(token_count * choice_count, dtype=jnp.int32) // choice_count
    payload_width = payload.shape[1]
    outgoing = (
        jnp.zeros((groups * capacity, payload_width), jnp.bfloat16)
        .at[target]
        .set(payload[source_row])
    )
    outgoing = outgoing.reshape(groups, capacity, payload_width)
    gate_matrix = gate_weight[0]
    up_matrix = up_weight[0]
    down_matrix = down_weight[0]
    arrived = lax.all_to_all(outgoing, "expert", split_axis=0, concat_axis=0, tiled=True)
    slot_count = arrived.shape[1]
    inputs = arrived.reshape(groups * slot_count, arrived.shape[2])
    gate_part = jnp.dot(inputs, gate_matrix, preferred_element_type=jnp.float32)
    up_part = jnp.dot(inputs, up_matrix, preferred_element_type=jnp.float32)
    activation = (jax.nn.silu(gate_part) * up_part).astype(jnp.bfloat16)
    answer = jnp.dot(
        lax.all_gather(activation, "hidden", axis=1, tiled=True),
        down_matrix,
        preferred_element_type=jnp.float32,
    ).astype(jnp.bfloat16)
    answer = answer.reshape(groups, slot_count, down_matrix.shape[1])
    returned_rows = lax.all_to_all(answer, "expert", split_axis=0, concat_axis=0, tiled=True)
    returned_rows = returned_rows.reshape(groups * capacity, returned_rows.shape[2])
    picked = returned_rows[target].astype(jnp.float32).reshape(token_count, choice_count, -1)
    combined = jnp.sum(picked * gates[:, :, None], axis=1).astype(jnp.bfloat16)
    combined_all = lax.all_gather(combined, "hidden", axis=1, tiled=True)
    columns = combined_all
    return jnp.dot(
        columns,
        lax.all_gather(dec_weight, "expert", axis=0, tiled=True),
        preferred_element_type=jnp.float32,
    ).astype(jnp.bfloat16)


def solution(mesh):
    in_specs = (
        P("expert", None),
        P("expert", "hidden"),
        P("expert", None),
        P("expert", None),
        P("expert", None, "hidden"),
        P("expert", None, "hidden"),
        P("expert", None, "hidden"),
        P("expert", "hidden"),
    )
    out_specs = P("expert", "hidden")
    return jax.shard_map(
        on_device, mesh=mesh, in_specs=in_specs, out_specs=out_specs, check_vma=False
    )
```

profile of v0, /device:TPU:0, one launch (start us, length us, event | category | flops | bytes accessed | tf_op | source)
XLA Modules:
  0.0 372.7 jit_solution(17849229389016442884)
XLA Ops:
  6.5 0.0 copy-start
  6.5 0.0 all-gather.4.cloned.1.call-start
  6.5 0.7 all-gather.4.cloned.1.call-update
  7.3 0.0 all-gather.6.cloned.1.call-start
  7.3 0.8 copy.13
  8.1 0.1 eq.29
  8.2 0.1 eq.25
  8.3 4.5 %reduce-window.6 = s32[16,8,128]{2,1,0:T(8,128)S(1)} reduce-window(s32[16,8,128]{2,1,0:T(8,128)S(1)} %fusion.11, s32[]{:T(128)} %constant.27.clone.1), window={size=1x1x128 pad=0_0x0_0x127_0}, to_apply=%region_0.0 | reduce-window | flops 2080768 | bytes 131076 | tf_op jit(solution)/shard_map/reduce-window
  12.8 0.1 slice.12
  12.9 0.1 copy.15
  13.1 0.1 copy.16
  13.1 0.7 broadcast_multiply_fusion
  13.8 0.1 copy.12
  13.9 0.1 mul.32
  14.0 0.1 broadcast_add_fusion
  14.2 48.4 %all-gather.4.cloned.1.call-done = bf16[4096,512]{1,0:T(8,128)(2,1)} async-done(((bf16[256,512]{1,0:T(8,128)(2,1)}), bf16[4096,512]{1,0:T(8,128)(2,1)}) %all-gather.4.cloned.1.call-update) | async-done | bytes 4194320 | tf_op jit(solution)/shard_map/all_gather | solution.py:14
  62.6 3.2 convolution_convert_fusion.2
  65.9 6.3 %all_gather.16 = bf16[128,1024]{1,0:T(8,128)(2,1)S(1)} all-gather(bf16[128,512]{1,0:T(8,128)(2,1)S(1)} %convolution_convert_fusion.2), channel_id=1, replica_groups=mesh['expert'=16,'hidden'=2] {'hidden'}, dimensions={1}, use_global_device_ids=true | all-gather | bytes 393216 | tf_op jit(solution)/shard_map/all_gather | solution.py:17
  72.2 15.3 %scatter_custom_fusion = bf16[2048,1024]{1,0:T(8,128)(2,1)} fusion(s32[1024]{0:T(1024)S(1)} %bitcast.51, bf16[128,1024]{1,0:T(8,128)(2,1)S(1)} %all_gather.16, s32[1024]{0:T(1024)S(1)} %broadcast_clamp_fusion.1, bf16[]{:T(256)} %constant.25.clone.1), kind=kCustom, calls=%fused_computation.8 | custom fusion | bytes 4194306 | tf_op jit(solution)/shard_map/scatter | solution.py:27
  87.4 95.8 %all_to_all.10 = bf16[16,128,1024]{2,1,0:T(8,128)(2,1)S(1)} all-to-all(bf16[16,128,1024]{2,1,0:T(8,128)(2,1)} %bitcast.44), channel_id=1, replica_groups=mesh['expert'=16,'hidden'=2] {'expert'}, dimensions={0} | all-to-all | bytes 8388608 | tf_op jit(solution)/shard_map/all_to_all | solution.py:33
  183.2 0.0 copy-done
  183.2 0.0 copy-start.2
  183.2 3.6 fusion.6
  186.8 0.0 copy-done.2
  186.8 0.0 copy-start.3
  186.8 5.4 %multiply_convert_fusion = bf16[2048,768]{1,0:T(8,128)(2,1)} fusion(f32[2048,768]{1,0:T(8,128)S(1)} %fusion.6, bf16[2048,1024]{1,0:T(8,128)(2,1)S(1)} %bitcast.46, bf16[1,1024,768]{2,1,0:T(8,128)(2,1)S(1)} %copy-done.2), kind=kOutput, calls=%fused_computation.3 | convolution fusion | flops 3230662656 | bytes 15204352 | tf_op jit(solution)/shard_map/dot_general | solution.py:37
  192.2 0.0 all-gather.6.cloned.1.call-update
  192.2 0.0 all-gather.8.cloned.1.call-start
  192.3 0.7 all-gather.8.cloned.1.call-update
  193.0 80.0 %all-gather.6.cloned.1.call-done = bf16[2048,1536]{1,0:T(8,128)(2,1)} async-done(((bf16[2048,768]{1,0:T(8,128)(2,1)}), bf16[2048,1536]{1,0:T(8,128)(2,1)}) %all-gather.6.cloned.1.call-update) | async-done | bytes 6291472 | tf_op jit(solution)/shard_map/all_gather | solution.py:40
  273.0 0.0 copy-done.3
  273.0 7.4 %convolution_convert_fusion = bf16[2048,512]{1,0:T(8,128)(2,1)} fusion(bf16[2048,1536]{1,0:T(8,128)(2,1)} %all-gather.6.cloned.1.call-done, bf16[1,1536,512]{2,1,0:T(8,128)(2,1)S(1)} %copy-done.3), kind=kOutput, calls=%fused_computation.4 | convolution fusion | flops 3222274048 | bytes 9961472 | tf_op jit(solution)/shard_map/dot_general | solution.py:39
  280.4 0.0 copy-start.1
  280.4 5.8 %all-to-all-start.1 = ((bf16[16,128,512]{2,1,0:T(8,128)(2,1)}), bf16[16,128,512]{2,1,0:T(8,128)(2,1)}, u32[]{:S(2)}, u32[]{:S(2)}) async-start(bf16[16,128,512]{2,1,0:T(8,128)(2,1)} %bitcast.47), calls=%async_computation.1 | async-start | bytes 4194304 | tf_op jit(solution)/shard_map/all_to_all | solution.py:45
  286.2 0.0 copy-done.1
  286.2 0.1 copy.17
  286.3 63.2 %all-to-all-done.1 = bf16[16,128,512]{2,1,0:T(8,128)(2,1)} async-done(((bf16[16,128,512]{2,1,0:T(8,128)(2,1)}), bf16[16,128,512]{2,1,0:T(8,128)(2,1)}, u32[]{:S(2)}, u32[]{:S(2)}) %all-to-all-start.1) | async-done | bytes 2097184 | tf_op jit(solution)/shard_map/all_to_all | solution.py:45
  349.5 5.8 %gather_fusion = bf16[1024,512]{1,0:T(8,128)(2,1)S(1)} fusion(bf16[2048,512]{1,0:T(8,128)(2,1)} %bitcast.11, s32[1024]{0:T(1024)S(1)} %broadcast_clamp_fusion), kind=kCustom, calls=%fused_computation.1 | custom fusion | bytes 2101248 | tf_op jit(solution)/shard_map/gather | solution.py:47
  355.4 0.7 fusion
  356.1 6.4 %all_gather.18 = bf16[128,1024]{1,0:T(8,128)(2,1)S(1)} all-gather(bf16[128,512]{1,0:T(8,128)(2,1)S(1)} %fusion), channel_id=1, replica_groups=mesh['expert'=16,'hidden'=2] {'hidden'}, dimensions={1}, use_global_device_ids=true | all-gather | bytes 393216 | tf_op jit(solution)/shard_map/all_gather | solution.py:49
  362.4 0.0 all-gather.8.cloned.1.call-done
  362.4 3.7 convolution_convert_fusion.1
  (8 shorter events, 0.1 us)
Async XLA Ops:
  6.5 176.7 %copy-start = (bf16[1,1024,768]{2,1,0:T(8,128)(2,1)S(1)}, bf16[1,1024,768]{2,1,0:T(8,128)(2,1)}, u32[]{:S(2)}) copy-start(bf16[1,1024,768]{2,1,0:T(8,128)(2,1)} %param.12) | copy-start | bytes 4718596
  6.5 56.1 %all-gather.4.cloned.1.call-start = ((), (), s32[]{:S(2)}) async-start(), calls=%async_computation.2 | async-start | bytes 4456448 | tf_op jit(solution)/shard_map/all_gather | solution.py:14
  7.3 265.7 %all-gather.6.cloned.1.call-start = ((), (), s32[]{:S(2)}) async-start(), calls=%async_computation.3 | async-start | bytes 9437184 | tf_op jit(solution)/shard_map/all_gather | solution.py:40
  183.2 3.6 copy-start.2
  186.8 86.1 %copy-start.3 = (bf16[1,1536,512]{2,1,0:T(8,128)(2,1)S(1)}, bf16[1,1536,512]{2,1,0:T(8,128)(2,1)}, u32[]{:S(2)}) copy-start(bf16[1,1536,512]{2,1,0:T(8,128)(2,1)} %param.14) | copy-start | bytes 4718596
  192.2 170.2 %all-gather.8.cloned.1.call-start = ((), (), s32[]{:S(2)}) async-start(), calls=%async_computation.4 | async-start | bytes 4456448 | tf_op jit(solution)/shard_map/all_gather | solution.py:53
  280.4 5.8 %copy-start.1 = (f32[128,8]{0,1:T(8,128)S(1)}, f32[128,8]{0,1:T(8,128)}, u32[]{:S(2)}) copy-start(f32[128,8]{0,1:T(8,128)} %param.11) | copy-start | bytes 12292
  280.4 69.1 %all-to-all-start.1 = ((bf16[16,128,512]{2,1,0:T(8,128)(2,1)}), bf16[16,128,512]{2,1,0:T(8,128)(2,1)}, u32[]{:S(2)}, u32[]{:S(2)}) async-start(bf16[16,128,512]{2,1,0:T(8,128)(2,1)} %bitcast.47), calls=%async_computation.1 | async-start | bytes 4194304 | tf_op jit(solution)/shard_map/all_to_all | solution.py:45
Sparse Core Ops, SparseCore 0:
  9.5 53.0 all-gather.3
  192.4 80.5 all-gather.5
  275.1 75.2 all-gather.7
where the time goes:
time: 378 us; the launch traced here: 373 us
  waiting for transfers between devices  193 us (51%)
  blocking collectives  108 us (29%)
  matrix products  23.3 us (6%)
  local copies, waits for them, and re-layouts  22.7 us (6%)
  between operations  13.2 us (3%)
  other arithmetic  6.08 us (2%)
  starting transfers between devices  5.88 us (2%)
    all_to_all x1, blocking collectives, on_device(): lax.all_to_all(outgoing, 'expert', split_axis=0, concat_axis=0, tiled=True)  95.8 us
    all_gather x1, waiting for transfers between devices, on_device(): lax.all_gather(activation, 'hidden', axis=1, tiled=True)  80 us
    all_to_all x1, waiting for transfers between devices, on_device(): lax.all_to_all(answer, 'expert', split_axis=0, concat_axis=0, tiled=True)  63.2 us
    all_gather x1, waiting for transfers between devices, on_device(): lax.all_gather(enc_weight, 'expert', axis=0, tiled=True)  48.4 us
    scatter x1, local copies, waits for them, and re-layouts, on_device(): outgoing = jnp.zeros((groups * capacity, payload_width), jnp.bfloat16).at...  15.3 us
  transfers between devices with their start and end apart: 4, of which 3 were waited for; matrix products, arithmetic and copies ran while one was open for 6% of the time, Pallas kernels for 0%

commit v1 on v0

--- a/solution.py
+++ b/solution.py
@@ -4,7 +4,7 @@
 from jax.sharding import PartitionSpec as P
 
 
-def on_device(tokens, enc_weight, routes, gates, gate_weight, up_weight, down_weight, dec_weight):
+def exchange_slots(tokens, enc_weight, routes, gates, gate_weight, up_weight, down_weight, dec_weight):
     groups = lax.axis_size("expert")
     token_count, choice_count = routes.shape
     capacity = min(token_count, 2 * token_count * choice_count // groups)
@@ -55,6 +55,39 @@
     ).astype(jnp.bfloat16)
 
 
+def every_token(tokens, enc_weight, routes, gates, gate_weight, up_weight, down_weight, dec_weight):
+    groups = lax.axis_size("expert")
+    latent = jnp.dot(
+        tokens,
+        lax.all_gather(enc_weight, "expert", axis=0, tiled=True),
+        preferred_element_type=jnp.float32,
+    ).astype(jnp.bfloat16)
+    payload = lax.all_gather(latent, "hidden", axis=1, tiled=True)
+    inputs = lax.all_gather(payload, "expert", axis=0, tiled=True)
+    onehot = routes[:, :, None] == jnp.arange(groups, dtype=jnp.int32)[None, None, :]
+    shares = jnp.sum(jnp.where(onehot, gates[:, :, None], 0.0), axis=1)
+    shares = lax.all_to_all(shares.T, "expert", split_axis=0, concat_axis=1, tiled=True)
+    down = lax.all_to_all(down_weight[0], "hidden", split_axis=0, concat_axis=1, tiled=True)
+    gate_part = jnp.dot(inputs, gate_weight[0], preferred_element_type=jnp.float32)
+    up_part = jnp.dot(inputs, up_weight[0], preferred_element_type=jnp.float32)
+    activation = (jax.nn.silu(gate_part) * up_part).astype(jnp.bfloat16)
+    answer = jnp.dot(activation, down, preferred_element_type=jnp.float32)
+    answer = (answer * shares.reshape(-1)[:, None]).astype(jnp.bfloat16)
+    combined = lax.psum_scatter(answer, "expert", scatter_dimension=0, tiled=True)
+    combined = lax.psum(combined, "hidden")
+    return jnp.dot(
+        combined,
+        lax.all_gather(dec_weight, "expert", axis=0, tiled=True),
+        preferred_element_type=jnp.float32,
+    ).astype(jnp.bfloat16)
+
+
+def on_device(tokens, enc_weight, routes, *rest):
+    token_count, choice_count = routes.shape
+    plan = every_token if 2 * choice_count >= lax.axis_size("expert") else exchange_slots
+    return plan(tokens, enc_weight, routes, *rest)
+
+
 def solution(mesh):
     in_specs = (
         P("expert", None),

time: 378 us -> 300 us (0.79); the launches traced: 373 us -> 300 us
  blocking collectives: 108 us -> 6.41 us
  waiting for transfers between devices: 193 us -> 243 us
  local copies, waits for them, and re-layouts: 22.7 us -> 1.59 us
  other arithmetic: 6.08 us -> 0.61 us
  matrix products: 23.3 us -> 28.4 us
    all_to_all x1 -> x0, blocking collectives: 95.8 us -> none  [on_device(): lax.all_to_all(outgoing, 'expert', split_axis=0, concat_axis=0, tiled=True)]
    reduce_scatter x0 -> x1, waiting for transfers between devices: none -> 70.8 us  [every_token(): lax.psum_scatter(answer, 'expert', scatter_dimension=0, tiled=True)]
    all_to_all x1 -> x2, waiting for transfers between devices: 63.2 us -> 18.4 us  [the longest x1 18.4 us: every_token(): lax.all_to_all(down_weight[0], 'hidden', split_axis=0, concat_axis=1, til...]
    psum x0 -> x1, waiting for transfers between devices: none -> 24 us  [every_token(): combined = lax.psum(combined, 'hidden')]
    scatter x1 -> x0, local copies, waits for them, and re-layouts: 15.3 us -> none  [on_device(): outgoing = jnp.zeros((groups * capacity, payload_width), jnp.bfloat16).at...]
    all_gather x2 -> x1, blocking collectives: 12.7 us -> 6.41 us  [every_token(): payload = lax.all_gather(latent, 'hidden', axis=1, tiled=True)]
    gather x1 -> x0, local copies, waits for them, and re-layouts: 5.85 us -> none  [on_device(): returned_rows[target].astype(jnp.float32)]
    dot_general x5 -> x4, matrix products: 23.3 us -> 28.4 us  [the longest x1 12.6 us: every_token(): answer = jnp.dot(activation, down, preferred_element_type=jnp.float32)]
  transfers between devices with their start and end apart: 4 -> 7, of which waited for: 3 -> 6; matrix products, arithmetic and copies ran while one was open for 6% -> 4% of each run, Pallas kernels for 0% -> 0%
where the time goes in v1:
time: 300 us
  waiting for transfers between devices  243 us (81%)
  matrix products  28.4 us (9%)
  between operations  13.2 us (4%)
  starting transfers between devices  7.32 us (2%)
  blocking collectives  6.41 us (2%)
    reduce_scatter x1, waiting for transfers between devices, every_token(): lax.psum_scatter(answer, 'expert', scatter_dimension=0, tiled=True)  70.8 us
    all_gather x1, waiting for transfers between devices, every_token(): lax.all_gather(enc_weight, 'expert', axis=0, tiled=True)  55.3 us
    all_gather x1, waiting for transfers between devices, every_token(): lax.all_gather(dec_weight, 'expert', axis=0, tiled=True)  51.5 us
    psum x1, waiting for transfers between devices, every_token(): combined = lax.psum(combined, 'hidden')  24 us
    all_gather x1, waiting for transfers between devices, every_token(): inputs = lax.all_gather(payload, 'expert', axis=0, tiled=True)  21.3 us
    all_to_all x1, waiting for transfers between devices, every_token(): lax.all_to_all(down_weight[0], 'hidden', split_axis=0, concat_axis=1, til...  18.4 us
    dot_general x1, matrix products, every_token(): answer = jnp.dot(activation, down, preferred_element_type=jnp.float32)  12.6 us
    dot_general x1, matrix products, every_token(): jnp.dot(inputs, gate_weight[0], preferred_element_type=jnp.float32)  8.75 us
  transfers between devices with their start and end apart: 7, of which 6 were waited for; matrix products, arithmetic and copies ran while one was open for 4% of the time, Pallas kernels for 0%

profile of v1, /device:TPU:0, one launch (start us, length us, event | category | flops | bytes accessed | tf_op | source)
XLA Modules:
  0.0 300.1 jit_solution(7086182725566540003)
XLA Ops:
  6.5 0.0 copy-start
  6.5 0.0 all-gather.4.cloned.1.call-start
  6.5 0.7 all-gather.4.cloned.1.call-update
  7.3 0.0 copy-start.2
  7.3 0.0 copy-start.3
  7.3 0.0 all-gather.6.cloned.1.call-start
  7.3 55.3 %all-gather.4.cloned.1.call-done = bf16[4096,512]{1,0:T(8,128)(2,1)} async-done(((bf16[256,512]{1,0:T(8,128)(2,1)}), bf16[4096,512]{1,0:T(8,128)(2,1)}) %all-gather.4.cloned.1.call-update) | async-done | bytes 4194320 | tf_op jit(solution)/shard_map/all_gather | solution.py:62
  62.6 3.2 %convolution_convert_fusion.1 = bf16[128,512]{1,0:T(8,128)(2,1)S(1)} fusion(bf16[128,4096]{1,0:T(8,128)(2,1)} %param.8, bf16[4096,512]{1,0:T(8,128)(2,1)} %all-gather.4.cloned.1.call-done), kind=kOutput, calls=%fused_computation.6 | convolution fusion | flops 536936448 | bytes 5373952 | tf_op jit(solution)/shard_map/dot_general | solution.py:60
  65.9 6.4 %all_gather.13 = bf16[128,1024]{1,0:T(8,128)(2,1)} all-gather(bf16[128,512]{1,0:T(8,128)(2,1)S(1)} %convolution_convert_fusion.1), channel_id=1, replica_groups=mesh['expert'=16,'hidden'=2] {'hidden'}, dimensions={1}, use_global_device_ids=true | all-gather | bytes 393216 | tf_op jit(solution)/shard_map/all_gather | solution.py:65
  72.3 0.0 all-gather.6.cloned.1.call-update
  72.3 3.7 %all-to-all-start = ((bf16[2,768,512]{2,1,0:T(8,128)(2,1)}), bf16[2,768,512]{2,1,0:T(8,128)(2,1)S(1)}, u32[]{:S(2)}, u32[]{:S(2)}) async-start(bf16[2,768,512]{2,1,0:T(8,128)(2,1)} %bitcast.24), calls=%async_computation | async-start | bytes 3145728 | tf_op jit(solution)/shard_map/all_to_all | solution.py:70
  76.0 0.0 copy-done.2
  76.0 0.0 copy-done.3
  76.0 0.6 select_reduce_fusion
  76.6 18.4 %all-to-all-done = bf16[2,768,512]{2,1,0:T(8,128)(2,1)S(1)} async-done(((bf16[2,768,512]{2,1,0:T(8,128)(2,1)}), bf16[2,768,512]{2,1,0:T(8,128)(2,1)S(1)}, u32[]{:S(2)}, u32[]{:S(2)}) %all-to-all-start) | async-done | bytes 1572896 | tf_op jit(solution)/shard_map/all_to_all | solution.py:70
  95.0 3.5 %all-to-all-start.1 = ((f32[16,1,128]{2,1,0:T(1,128)}), f32[16,1,128]{2,1,0:T(1,128)S(1)}, u32[]{:S(2)}, u32[]{:S(2)}) async-start(f32[16,1,128]{2,1,0:T(1,128)} %bitcast.7), calls=%async_computation.1 | async-start | bytes 16384 | tf_op jit(solution)/shard_map/all_to_all | solution.py:69
  98.5 0.0 reduce-scatter.2.cloned.1.call-start
  98.5 1.6 copy.19
  100.1 0.0 copy-start.1
  100.1 21.3 %all-gather.6.cloned.1.call-done = bf16[2048,1024]{1,0:T(8,128)(2,1)} async-done(((bf16[128,1024]{1,0:T(8,128)(2,1)}), bf16[2048,1024]{1,0:T(8,128)(2,1)}) %all-gather.6.cloned.1.call-update) | async-done | bytes 4194320 | tf_op jit(solution)/shard_map/all_gather | solution.py:66
  121.5 8.8 %fusion.2 = f32[2048,768]{1,0:T(8,128)} fusion(bf16[2048,1024]{1,0:T(8,128)(2,1)} %all-gather.6.cloned.1.call-done, bf16[1,1024,768]{2,1,0:T(8,128)(2,1)} %param.12), kind=kOutput, calls=%fused_computation.4 | convolution fusion | flops 3221225472 | bytes 12058624 | tf_op jit(solution)/shard_map/dot_general | solution.py:71
  130.2 0.0 all-to-all-done.1
  130.2 0.0 copy-done
  130.2 0.0 copy-done.1
  130.2 12.6 %multiply_convert_fusion = bf16[2048,1024]{1,0:T(8,128)(2,1)} fusion(bf16[768,1024]{0,1:T(8,128)(2,1)S(1)} %bitcast.25, f32[2048]{0:T(1024)S(1)} %bitcast.26, f32[2048,768]{1,0:T(8,128)} %fusion.2, bf16[2048,1024]{1,0:T(8,128)(2,1)} %all-gather.6.cloned.1.call-done, bf16[1,1024,768]{2,1,0:T(8,128)(2,1)S(1)} %copy-done), kind=kOutput, calls=%fused_computation | convolution fusion | flops 6456082432 | bytes 17833984 | tf_op jit(solution)/shard_map/dot_general | solution.py:74
  142.8 0.0 reduce-scatter.2.cloned.1.call-update
  142.8 0.0 all-gather.8.cloned.1.call-start
  142.9 0.5 all-gather.8.cloned.1.call-update
  143.4 0.0 all-reduce.2.cloned.1.call-start
  143.5 70.8 %reduce-scatter.2.cloned.1.call-done = bf16[128,1024]{1,0:T(8,128)(2,1)} async-done(((bf16[2048,1024]{1,0:T(8,128)(2,1)}), bf16[128,1024]{1,0:T(8,128)(2,1)}) %reduce-scatter.2.cloned.1.call-update) | async-done | bytes 262160 | tf_op jit(solution)/shard_map/reduce_scatter | solution.py:76
  214.3 0.0 all-reduce.2.cloned.1.call-update
  214.3 51.5 %all-gather.8.cloned.1.call-done = bf16[1024,2048]{1,0:T(8,128)(2,1)} async-done(((bf16[64,2048]{1,0:T(8,128)(2,1)}), bf16[1024,2048]{1,0:T(8,128)(2,1)}) %all-gather.8.cloned.1.call-update) | async-done | bytes 4194320 | tf_op jit(solution)/shard_map/all_gather | solution.py:80
  265.8 24.0 %all-reduce.2.cloned.1.call-done = bf16[128,1024]{1,0:T(8,128)(2,1)} async-done(((bf16[128,1024]{1,0:T(8,128)(2,1)}), bf16[128,1024]{1,0:T(8,128)(2,1)}) %all-reduce.2.cloned.1.call-update) | async-done | bytes 262160 | tf_op jit(solution)/shard_map/psum | solution.py:77
  289.8 3.8 %convolution_convert_fusion = bf16[128,2048]{1,0:T(8,128)(2,1)} fusion(bf16[128,1024]{1,0:T(8,128)(2,1)} %all-reduce.2.cloned.1.call-done, bf16[1024,2048]{1,0:T(8,128)(2,1)} %all-gather.8.cloned.1.call-done), kind=kOutput, calls=%fused_computation.2 | convolution fusion | flops 537133056 | bytes 4980736 | tf_op jit(solution)/shard_map/dot_general | solution.py:78
Async XLA Ops:
  6.5 123.7 %copy-start = (bf16[1,1024,768]{2,1,0:T(8,128)(2,1)S(1)}, bf16[1,1024,768]{2,1,0:T(8,128)(2,1)}, u32[]{:S(2)}) copy-start(bf16[1,1024,768]{2,1,0:T(8,128)(2,1)} %param.13) | copy-start | bytes 4718596
  6.5 56.1 %all-gather.4.cloned.1.call-start = ((), (), s32[]{:S(2)}) async-start(), calls=%async_computation.3 | async-start | bytes 4456448 | tf_op jit(solution)/shard_map/all_gather | solution.py:62
  7.3 68.7 %copy-start.2 = (f32[128,8]{0,1:T(8,128)S(1)}, f32[128,8]{0,1:T(8,128)}, u32[]{:S(2)}) copy-start(f32[128,8]{0,1:T(8,128)} %param.11) | copy-start | bytes 12292
  7.3 68.7 %copy-start.3 = (s32[128,8]{0,1:T(8,128)S(1)}, s32[128,8]{0,1:T(8,128)}, u32[]{:S(2)}) copy-start(s32[128,8]{0,1:T(8,128)} %param.10) | copy-start | bytes 12292
  7.3 114.2 %all-gather.6.cloned.1.call-start = ((), (), s32[]{:S(2)}) async-start(), calls=%async_computation.4 | async-start | bytes 4456448 | tf_op jit(solution)/shard_map/all_gather | solution.py:66
  72.3 22.7 %all-to-all-start = ((bf16[2,768,512]{2,1,0:T(8,128)(2,1)}), bf16[2,768,512]{2,1,0:T(8,128)(2,1)S(1)}, u32[]{:S(2)}, u32[]{:S(2)}) async-start(bf16[2,768,512]{2,1,0:T(8,128)(2,1)} %bitcast.24), calls=%async_computation | async-start | bytes 3145728 | tf_op jit(solution)/shard_map/all_to_all | solution.py:70
  95.0 35.2 %all-to-all-start.1 = ((f32[16,1,128]{2,1,0:T(1,128)}), f32[16,1,128]{2,1,0:T(1,128)S(1)}, u32[]{:S(2)}, u32[]{:S(2)}) async-start(f32[16,1,128]{2,1,0:T(1,128)} %bitcast.7), calls=%async_computation.1 | async-start | bytes 16384 | tf_op jit(solution)/shard_map/all_to_all | solution.py:69
  98.5 115.8 %reduce-scatter.2.cloned.1.call-start = ((), (), s32[]{:S(2)}) async-start(), calls=%async_computation.5 | async-start | bytes 4456448 | tf_op jit(solution)/shard_map/reduce_scatter | solution.py:76
  100.1 30.1 %copy-start.1 = (bf16[768,2,512]{0,2,1:T(8,128)(2,1)S(1)}, bf16[768,2,512]{0,2,1:T(8,128)(2,1)}, u32[]{:S(2)}) copy-start(bf16[768,2,512]{0,2,1:T(8,128)(2,1)} %copy.19) | copy-start | bytes 4718596
  142.8 123.0 %all-gather.8.cloned.1.call-start = ((), (), s32[]{:S(2)}) async-start(), calls=%async_computation.7 | async-start | bytes 4456448 | tf_op jit(solution)/shard_map/all_gather | solution.py:80
  143.4 146.4 %all-reduce.2.cloned.1.call-start = ((), (), s32[]{:S(2)}) async-start(), calls=%async_computation.6 | async-start | bytes 524288 | tf_op jit(solution)/shard_map/psum | solution.py:77
Sparse Core Ops, SparseCore 0:
  9.5 53.0 all-gather.3
  72.4 48.9 all-gather.5
  143.0 71.2 reduce-scatter.1
  216.3 49.4 all-gather.7
  267.9 21.8 all-reduce.1

commit v2 on v0

--- a/solution.py
+++ b/solution.py
@@ -1,10 +1,12 @@
 import jax
 import jax.numpy as jnp
 from jax import lax
+from jax.experimental import pallas as pl
+from jax.experimental.pallas import tpu as pltpu
 from jax.sharding import PartitionSpec as P
 
 
-def on_device(tokens, enc_weight, routes, gates, gate_weight, up_weight, down_weight, dec_weight):
+def exchange_slots(tokens, enc_weight, routes, gates, gate_weight, up_weight, down_weight, dec_weight):
     groups = lax.axis_size("expert")
     token_count, choice_count = routes.shape
     capacity = min(token_count, 2 * token_count * choice_count // groups)
@@ -55,6 +57,373 @@
     ).astype(jnp.bfloat16)
 
 
+CORES, LINES = 2, 2
+MESH = pl.DeviceIdType.MESH
+
+
+def layer_kernel(
+    tokens_hbm, enc, gate_hbm, up_hbm, down_hbm, dec, out,
+    tokens, gate, up, down, enc_all, dec_all, latents, shares, activation,
+    answers, core_in, x_out, x_in, keep, y_out, y_in, z_out, z_in, combined,
+    enc_recv, enc_send, lat_recv, lat_send, dec_recv, dec_send,
+    down_recv, down_send, core_recv, core_send, x_recv, x_send, y_recv, y_send,
+    z_recv, z_send, last_recv, last_send, local_sem,
+):
+    groups = lax.axis_size("expert")
+    depth = groups // (CORES * LINES)
+    e = lax.axis_index("expert")
+    h = lax.axis_index("hidden")
+    c, y, z = e % CORES, (e // CORES) % LINES, e // (CORES * LINES)
+
+    def at(zz, yy, cc):
+        return (zz * LINES + yy) * CORES + cc
+
+    def behind(s):
+        return (z + depth - s) % depth
+
+    rows = tokens.shape[0]
+    half = latents.shape[2]
+    enc_rows = tokens.shape[1] // groups
+    band = LINES * CORES * rows
+    y_peer = (at(z, 1 - y, c), h)
+    core_peer = (at(z, y, 1 - c), h)
+    x_peer = (e, 1 - h)
+    z_peers = [(at((z + s) % depth, y, c), h) for s in range(1, depth)]
+
+    waiting = []
+
+    def send(src, dst, ssem, rsem, peer):
+        copy = pltpu.make_async_remote_copy(
+            src_ref=src, dst_ref=dst, send_sem=ssem, recv_sem=rsem,
+            device_id=peer, device_id_type=MESH,
+        )
+        copy.start()
+        waiting.append(copy)
+
+    def arrive(dst, rsem):
+        pltpu.make_async_copy(dst, dst, rsem).wait()
+
+    barrier = pltpu.get_barrier_semaphore()
+    peers = z_peers + [y_peer, core_peer, x_peer]
+    for peer in peers:
+        pl.semaphore_signal(barrier, inc=1, device_id=peer, device_id_type=MESH)
+    pl.semaphore_wait(barrier, len(peers))
+
+    class Gather:
+        def __init__(self, own, buffer, rsem, ssem):
+            self.own, self.buffer, self.rsem, self.ssem = own, buffer, rsem, ssem
+
+        def forward(self, o, peer, slot, own=False):
+            src = self.own if own else self.buffer.at[o]
+            send(src, self.buffer.at[o], self.ssem.at[slot], self.rsem.at[o], peer)
+
+        def wait(self, o):
+            arrive(self.buffer.at[o], self.rsem.at[o])
+
+        def start(self):
+            for s in range(1, depth):
+                self.forward(e, z_peers[s - 1], s - 1, True)
+            self.forward(e, y_peer, depth - 1, True)
+            self.forward(e, core_peer, 2 * depth - 1, True)
+
+        def from_z(self, s):
+            o = at(behind(s), y, c)
+            self.wait(o)
+            self.forward(o, y_peer, depth - 1 + s)
+            self.forward(o, core_peer, 2 * depth - 1 + s)
+            return o
+
+        def from_y(self, s):
+            o = at(behind(s), 1 - y, c)
+            self.wait(o)
+            self.forward(o, core_peer, 3 * depth - 1 + s)
+            return o
+
+        def from_core(self, s, yy):
+            o = at(behind(s), yy, 1 - c)
+            self.wait(o)
+            return o
+
+    enc_gather = Gather(enc, enc_all, enc_recv, enc_send)
+    dec_gather = Gather(dec, dec_all, dec_recv, dec_send)
+    enc_gather.start()
+
+    local = [
+        pltpu.make_async_copy(tokens_hbm, tokens, local_sem.at[0]),
+        pltpu.make_async_copy(gate_hbm.at[0], gate, local_sem.at[1]),
+        pltpu.make_async_copy(up_hbm.at[0], up, local_sem.at[2]),
+    ]
+    for copy in local:
+        copy.start()
+    part = down.shape[1]
+    own_down = pltpu.make_async_copy(
+        down_hbm.at[0, pl.ds(pl.multiple_of(h * part, part), part)], down.at[h], local_sem.at[3]
+    )
+    own_down.start()
+    send(
+        down_hbm.at[0, pl.ds(pl.multiple_of((1 - h) * part, part), part)],
+        down.at[h], down_send.at[0], down_recv.at[0], x_peer,
+    )
+
+    local[0].wait()
+
+    def enc_dot(o, block):
+        columns = pl.ds(pl.multiple_of(o * enc_rows, enc_rows), enc_rows)
+        return jnp.dot(tokens[:, columns], block[:enc_rows], preferred_element_type=jnp.float32)
+
+    def take_shares(o, block):
+        pieces = half // 128
+        piece = rows // pieces
+        for q in range(pieces):
+            tile = block[enc_rows:, q * 128 : (q + 1) * 128].astype(jnp.float32)
+            lane = lax.broadcasted_iota(jnp.int32, tile.shape, 1)
+            mine = jnp.logical_and(lane % groups == e, lane < 3 * groups)
+            total = jnp.sum(jnp.where(mine, tile, 0.0), axis=1, keepdims=True)
+            start = pl.multiple_of(o * rows + q * piece, piece)
+            shares[pl.ds(start, piece), :] = jnp.broadcast_to(total, (piece, 128))
+
+    total = enc_dot(e, enc[...])
+    take_shares(e, enc[...])
+
+    def landed(o, total):
+        take_shares(o, enc_all[o])
+        return total + enc_dot(o, enc_all[o])
+
+    for s in range(1, depth + 1):
+        if s < depth:
+            total = landed(enc_gather.from_z(s), total)
+        total = landed(enc_gather.from_y(s - 1), total)
+    for s in range(depth):
+        total = landed(enc_gather.from_core(s, y), total)
+    for s in range(depth):
+        total = landed(enc_gather.from_core(s, 1 - y), total)
+
+    def lat(hh, o):
+        return latents.at[hh, pl.ds(pl.multiple_of(o * rows, rows), rows)]
+
+    def lat_forward(hh, o, peer, slot):
+        send(lat(hh, o), lat(hh, o), lat_send.at[slot], lat_recv.at[hh, o], peer)
+
+    def lat_wait(hh, o):
+        arrive(lat(hh, o), lat_recv.at[hh, o])
+
+    latents[h, pl.ds(pl.multiple_of(e * rows, rows), rows), :] = total.astype(jnp.bfloat16)
+    base_y, base_x, base_c = depth, 2 * depth, 4 * depth
+    for s in range(1, depth):
+        lat_forward(h, e, z_peers[s - 1], s - 1)
+    lat_forward(h, e, y_peer, base_y)
+    lat_forward(h, e, x_peer, base_x)
+    lat_forward(h, e, core_peer, base_c)
+
+    def lat_z(s):
+        o = at(behind(s), y, c)
+        lat_wait(h, o)
+        lat_forward(h, o, y_peer, base_y + s)
+        lat_forward(h, o, x_peer, base_x + s)
+        lat_forward(h, o, core_peer, base_c + s)
+
+    def lat_y(s):
+        o = at(behind(s), 1 - y, c)
+        lat_wait(h, o)
+        lat_forward(h, o, x_peer, base_x + depth + s)
+        lat_forward(h, o, core_peer, base_c + depth + s)
+
+    def lat_x(s):
+        for k, yy in enumerate((y, 1 - y)):
+            o = at(behind(s), yy, c)
+            lat_wait(1 - h, o)
+            lat_forward(1 - h, o, core_peer, base_c + (2 + k) * depth + s)
+
+    def lat_core(s):
+        for hh in (h, 1 - h):
+            for yy in (y, 1 - y):
+                lat_wait(hh, at(behind(s), yy, 1 - c))
+
+    tile = 256
+
+    def experts(s):
+        start = pl.multiple_of(behind(s) * band, band)
+
+        @pl.loop(0, gate.shape[1] // tile)
+        def _(n):
+            columns = pl.ds(pl.multiple_of(n * tile, tile), tile)
+            low, high = latents[0, pl.ds(start, band), :], latents[1, pl.ds(start, band), :]
+            g = jnp.dot(low, gate[:half, columns], preferred_element_type=jnp.float32)
+            g += jnp.dot(high, gate[half:, columns], preferred_element_type=jnp.float32)
+            u = jnp.dot(low, up[:half, columns], preferred_element_type=jnp.float32)
+            u += jnp.dot(high, up[half:, columns], preferred_element_type=jnp.float32)
+            activation[:, columns] = (g / (1.0 + jnp.exp(-g)) * u).astype(jnp.bfloat16)
+
+        for hh in range(2):
+            @pl.loop(0, half // tile)
+            def _(n):
+                columns = pl.ds(pl.multiple_of(n * tile, tile), tile)
+                a = jnp.dot(activation[...], down[hh, :, columns], preferred_element_type=jnp.float32)
+                a = (a * shares[pl.ds(start, band), 0:1]).astype(jnp.bfloat16)
+                for b in range(LINES * CORES):
+                    answers[s, b, hh, :, columns] = a[b * rows : (b + 1) * rows]
+
+        for yy in range(LINES):
+            send(
+                answers.at[s, yy * CORES + 1 - c], core_in.at[s, yy],
+                core_send.at[s, yy], core_recv.at[s, yy], core_peer,
+            )
+
+    def sum_cores(s):
+        for yy in range(LINES):
+            arrive(core_in.at[s, yy], core_recv.at[s, yy])
+            mine = yy * CORES + c
+            other = answers[s, mine, 1 - h].astype(jnp.float32)
+            x_out[s, yy] = (other + core_in[s, yy, 1 - h].astype(jnp.float32)).astype(jnp.bfloat16)
+        send(x_out.at[s], x_in.at[s], x_send.at[s], x_recv.at[s], x_peer)
+        for yy in range(LINES):
+            mine = yy * CORES + c
+            keep[s, yy] = answers[s, mine, h].astype(jnp.float32) + core_in[s, yy, h].astype(jnp.float32)
+
+    def sum_x(s):
+        arrive(x_in.at[s], x_recv.at[s])
+        y_out[s] = (keep[s, 1 - y] + x_in[s, 1 - y].astype(jnp.float32)).astype(jnp.bfloat16)
+        send(y_out.at[s], y_in.at[s], y_send.at[s], y_recv.at[s], y_peer)
+        keep[s, y] = keep[s, y] + x_in[s, y].astype(jnp.float32)
+
+    def sum_y(s):
+        arrive(y_in.at[s], y_recv.at[s])
+        total = keep[s, y] + y_in[s].astype(jnp.float32)
+        if s == 0:
+            keep[s, y] = total
+        else:
+            z_out[s] = total.astype(jnp.bfloat16)
+            peer = (at(behind(s), y, c), h)
+            send(z_out.at[s], z_in.at[s], z_send.at[s], z_recv.at[s], peer)
+
+    for s in range(1, depth + 1):
+        if s < depth:
+            lat_z(s)
+        lat_y(s - 1)
+    dec_gather.start()
+    local[1].wait()
+    local[2].wait()
+    own_down.wait()
+    arrive(down.at[1 - h], down_recv.at[0])
+    for s in range(depth):
+        lat_x(s)
+        lat_core(s)
+        experts(s)
+        if s >= 1:
+            sum_cores(s - 1)
+        if s >= 2:
+            sum_x(s - 2)
+        if s >= 3:
+            sum_y(s - 3)
+        if s == 0:
+            for k in range(1, depth):
+                dec_gather.from_z(k)
+        if s == 1:
+            for k in range(depth):
+                dec_gather.from_y(k)
+    for s in range(depth, depth + 3):
+        if s - 1 < depth:
+            sum_cores(s - 1)
+        if 0 <= s - 2 < depth:
+            sum_x(s - 2)
+        if 0 <= s - 3 < depth:
+            sum_y(s - 3)
+    final = keep[0, y]
+    for s in range(1, depth):
+        arrive(z_in.at[s], z_recv.at[s])
+        final += z_in[s].astype(jnp.float32)
+    combined[h] = final.astype(jnp.bfloat16)
+    send(combined.at[h], combined.at[h], last_send.at[0], last_recv.at[0], x_peer)
+    for s in range(depth):
+        for yy in (y, 1 - y):
+            dec_gather.from_core(s, yy)
+    dec_all[e] = dec[...]
+    arrive(combined.at[1 - h], last_recv.at[0])
+
+    per = groups // 2
+
+    @pl.loop(0, out.shape[1] // tile)
+    def _(n):
+        columns = pl.ds(pl.multiple_of(n * tile, tile), tile)
+        low = dec_all[:per, :, columns].reshape(half, tile)
+        high = dec_all[per:, :, columns].reshape(half, tile)
+        m = jnp.dot(combined[0], low, preferred_element_type=jnp.float32)
+        m += jnp.dot(combined[1], high, preferred_element_type=jnp.float32)
+        out[:, columns] = m.astype(jnp.bfloat16)
+
+    for copy in waiting:
+        copy.wait_send()
+
+
+def whole_layer(tokens, enc_weight, routes, gates, gate_weight, up_weight, down_weight, dec_weight):
+    groups = lax.axis_size("expert")
+    depth = groups // (CORES * LINES)
+    rows, width = tokens.shape
+    enc_rows, half = enc_weight.shape
+    hidden = gate_weight.shape[2]
+    onehot = routes[:, :, None] == jnp.arange(groups, dtype=jnp.int32)[None, None, :]
+    rest = jnp.sum(jnp.where(onehot, gates[:, :, None], 0.0), axis=1)
+    parts = []
+    for _ in range(3):
+        piece = lax.reduce_precision(rest, 8, 7)
+        parts.append(piece.astype(jnp.bfloat16))
+        rest = rest - piece
+    packed = jnp.concatenate(parts, axis=1)
+    packed = jnp.pad(packed, ((0, 0), (0, 128 - packed.shape[1])))
+    pieces = half // 128
+    packed = packed.reshape(pieces, rows // pieces, 128).transpose(1, 0, 2).reshape(-1, half)
+    enc = jnp.concatenate([enc_weight, packed], axis=0)
+    bf, f32 = jnp.bfloat16, jnp.float32
+    band = LINES * CORES
+    anywhere = pl.BlockSpec(memory_space=pl.ANY)
+    vmem = pl.BlockSpec(memory_space=pltpu.VMEM)
+    dma = pltpu.SemaphoreType.DMA
+    scratch = [
+        pltpu.VMEM((rows, width), bf),
+        pltpu.VMEM(gate_weight.shape[1:], bf),
+        pltpu.VMEM(up_weight.shape[1:], bf),
+        pltpu.VMEM((2, hidden, half), bf),
+        pltpu.VMEM((groups, *enc.shape), bf),
+        pltpu.VMEM((groups, *dec_weight.shape), bf),
+        pltpu.VMEM((2, groups * rows, half), bf),
+        pltpu.VMEM((groups * rows, 128), f32),
+        pltpu.VMEM((band * rows, hidden), bf),
+        pltpu.VMEM((depth, band, 2, rows, half), bf),
+        pltpu.VMEM((depth, LINES, 2, rows, half), bf),
+        pltpu.VMEM((depth, LINES, rows, half), bf),
+        pltpu.VMEM((depth, LINES, rows, half), bf),
+        pltpu.VMEM((depth, LINES, rows, half), f32),
+        pltpu.VMEM((depth, rows, half), bf),
+        pltpu.VMEM((depth, rows, half), bf),
+        pltpu.VMEM((depth, rows, half), bf),
+        pltpu.VMEM((depth, rows, half), bf),
+        pltpu.VMEM((2, rows, half), bf),
+        dma((groups,)), dma((4 * depth,)),
+        dma((2, groups)), dma((8 * depth,)),
+        dma((groups,)), dma((4 * depth,)),
+        dma((1,)), dma((1,)),
+        dma((depth, LINES)), dma((depth, LINES)),
+        dma((depth,)), dma((depth,)), dma((depth,)), dma((depth,)), dma((depth,)), dma((depth,)),
+        dma((1,)), dma((1,)), dma((4,)),
+    ]
+    return pl.pallas_call(
+        layer_kernel,
+        out_shape=jax.ShapeDtypeStruct((rows, dec_weight.shape[1]), bf),
+        in_specs=[anywhere, vmem, anywhere, anywhere, anywhere, vmem],
+        out_specs=vmem,
+        scratch_shapes=scratch,
+        compiler_params=pltpu.CompilerParams(
+            collective_id=0, has_side_effects=True, vmem_limit_bytes=60 * 1024 * 1024
+        ),
+    )(tokens, enc, gate_weight, up_weight, down_weight, dec_weight)
+
+
+def on_device(tokens, enc_weight, routes, *rest):
+    token_count, choice_count = routes.shape
+    plan = whole_layer if 2 * choice_count >= lax.axis_size("expert") else exchange_slots
+    return plan(tokens, enc_weight, routes, *rest)
+
+
 def solution(mesh):
     in_specs = (
         P("expert", None),

time: 378 us -> 145 us (0.38); the launches traced: 373 us -> 145 us
  waiting for transfers between devices: 193 us -> 0 us
  Pallas kernels: 0 us -> 140 us
  blocking collectives: 108 us -> 0 us
  matrix products: 23.3 us -> 0 us
  local copies, waits for them, and re-layouts: 22.7 us -> 2.02 us
  between operations: 13.2 us -> 0.04 us
  starting transfers between devices: 5.88 us -> 0 us
    pallas_call x0 -> x1, Pallas kernels: none -> 140 us  [whole_layer(): pl.pallas_call(layer_kernel, out_shape=jax.ShapeDtypeStruct((rows, dec_we...]
    all_gather x3 -> x0, waiting for transfers between devices: 128 us -> none  [the longest x1 80 us: on_device(): lax.all_gather(activation, 'hidden', axis=1, tiled=True)]
    all_to_all x1 -> x0, blocking collectives: 95.8 us -> none  [on_device(): lax.all_to_all(outgoing, 'expert', split_axis=0, concat_axis=0, tiled=True)]
    all_to_all x1 -> x0, waiting for transfers between devices: 63.2 us -> none  [on_device(): lax.all_to_all(answer, 'expert', split_axis=0, concat_axis=0, tiled=True)]
    dot_general x5 -> x0, matrix products: 23.3 us -> none  [the longest x1 7.43 us: on_device(): jnp.dot(lax.all_gather(activation, 'hidden', axis=1, tiled=True), down_ma...]
    scatter x1 -> x0, local copies, waits for them, and re-layouts: 15.3 us -> none  [on_device(): outgoing = jnp.zeros((groups * capacity, payload_width), jnp.bfloat16).at...]
    all_gather x2 -> x0, blocking collectives: 12.7 us -> none  [the longest x1 6.38 us: on_device(): combined_all = lax.all_gather(combined, 'hidden', axis=1, tiled=True)]
    gather x1 -> x0, local copies, waits for them, and re-layouts: 5.85 us -> none  [on_device(): returned_rows[target].astype(jnp.float32)]
  transfers between devices with their start and end apart: 4 -> 0, of which waited for: 3 -> 0; matrix products, arithmetic and copies ran while one was open for 6% -> 0% of each run, Pallas kernels for 0% -> 0%
where the time goes in v2:
time: 145 us
  Pallas kernels  140 us (97%)
  other arithmetic  2.42 us (2%)
  local copies, waits for them, and re-layouts  2.02 us (1%)
    pallas_call x1, Pallas kernels, whole_layer(): pl.pallas_call(layer_kernel, out_shape=jax.ShapeDtypeStruct((rows, dec_we...  140 us

profile of v2, /device:TPU:0, one launch (start us, length us, event | category | flops | bytes accessed | tf_op | source)
XLA Modules:
  0.0 144.8 jit_solution(10708320622458385044)
XLA Ops:
  0.0 0.7 select_reduce_fusion
  0.7 0.1 copy.18
  0.9 1.7 %pad_maximum_fusion.enc = bf16[288,512]{1,0:T(8,128)(2,1)} fusion(bf16[32,512]{1,0:T(8,128)(2,1)S(1)} %bitcast.7, bf16[256,512]{1,0:T(8,128)(2,1)} %param.9), kind=kLoop, calls=%fused_computation | loop fusion | flops 589824 | bytes 589824 | tf_op jit(solution)/shard_map/concatenate | solution.py:375
  2.6 140.3 %shard_map.82 = bf16[128,2048]{1,0:T(8,128)(2,1)} custom-call(bf16[128,4096]{1,0:T(8,128)(2,1)} %tokens_hbm.1, bf16[288,512]{1,0:T(8,128)(2,1)} %pad_maximum_fusion.enc, bf16[1,1024,768]{2,1,0:T(8,128)(2,1)} %gate_hbm.1, bf16[1,1024,768]{2,1,0:T(8,128)(2,1)} %up_hbm.1, bf16[1,1536,512]{2,1,0:T(8,128)(2,1)} %down_hbm.1, bf16[64,2048]{1,0:T(8,128)(2,1)} %dec.1), custom_call_target="tpu_custom_call" | custom-call | tf_op jit(solution)/shard_map/pallas_call | solution.py:409
  142.9 1.9 %copy.24 = bf16[128,2048]{1,0:T(8,128)(2,1)} copy(bf16[128,2048]{1,0:T(8,128)(2,1)} %shard_map.82) | data formatting | bytes 1048576
  (4 shorter events, 0.0 us)

commit v3 on v2

--- a/solution.py
+++ b/solution.py
@@ -62,11 +62,12 @@
 
 
 def layer_kernel(
-    tokens_hbm, enc, gate_hbm, up_hbm, down_hbm, dec, out,
-    tokens, gate, up, down, enc_all, dec_all, latents, shares, activation,
+    tokens_hbm, enc, routes, gates, gate_hbm, up_hbm, down_hbm, dec, out,
+    tokens, gate, up, down, enc_all, dec_all, latents, own_pack, pack_all, shares, total, activation,
     answers, core_in, x_out, x_in, keep, y_out, y_in, z_out, z_in, combined,
     enc_recv, enc_send, lat_recv, lat_send, dec_recv, dec_send,
-    down_recv, down_send, core_recv, core_send, x_recv, x_send, y_recv, y_send,
+    pack_recv, pack_send,
+    down_recv, down_send, core_recv, core_send, x_lat_recv, x_lat_send, core_lat_recv, core_lat_send, x_recv, x_send, y_recv, y_send,
     z_recv, z_send, last_recv, last_send, local_sem,
 ):
     groups = lax.axis_size("expert")
@@ -78,8 +79,19 @@
     def at(zz, yy, cc):
         return (zz * LINES + yy) * CORES + cc
 
+    orders = []
+    for zz in range(depth):
+        others = [o for o in range(depth) if o != zz]
+        orders.append([zz] + sorted(others, key=lambda o: (abs(o - zz), o)))
+    nearest = []
+    for s in range(depth):
+        pick = jnp.int32(orders[0][s])
+        for zz in range(1, depth):
+            pick = jnp.where(z == zz, orders[zz][s], pick)
+        nearest.append(pick)
+
     def behind(s):
-        return (z + depth - s) % depth
+        return nearest[s]
 
     rows = tokens.shape[0]
     half = latents.shape[2]
@@ -89,16 +101,22 @@
     core_peer = (at(z, y, 1 - c), h)
     x_peer = (e, 1 - h)
     z_peers = [(at((z + s) % depth, y, c), h) for s in range(1, depth)]
+    above = (at(jnp.minimum(z + 1, depth - 1), y, c), h)
+    below = (at(jnp.maximum(z - 1, 0), y, c), h)
+    has_above, has_below = z < depth - 1, z > 0
 
     waiting = []
 
-    def send(src, dst, ssem, rsem, peer):
+    def send(src, dst, ssem, rsem, peer, when=None):
         copy = pltpu.make_async_remote_copy(
             src_ref=src, dst_ref=dst, send_sem=ssem, recv_sem=rsem,
             device_id=peer, device_id_type=MESH,
         )
-        copy.start()
-        waiting.append(copy)
+        if when is None:
+            copy.start()
+        else:
+            pl.when(when)(copy.start)
+        waiting.append((copy, when))
 
     def arrive(dst, rsem):
         pltpu.make_async_copy(dst, dst, rsem).wait()
@@ -110,43 +128,66 @@
     pl.semaphore_wait(barrier, len(peers))
 
     class Gather:
-        def __init__(self, own, buffer, rsem, ssem):
-            self.own, self.buffer, self.rsem, self.ssem = own, buffer, rsem, ssem
-
-        def forward(self, o, peer, slot, own=False):
-            src = self.own if own else self.buffer.at[o]
-            send(src, self.buffer.at[o], self.ssem.at[slot], self.rsem.at[o], peer)
+        def __init__(self, own, block, rsem, ssem):
+            self.own, self.block, self.rsem, self.ssem = own, block, rsem, ssem
+
+        def forward(self, o, peer, slot, own=False, when=None):
+            src = self.own if own else self.block(o)
+            send(src, self.block(o), self.ssem.at[slot], self.rsem.at[o], peer, when)
 
         def wait(self, o):
-            arrive(self.buffer.at[o], self.rsem.at[o])
-
-        def start(self):
-            for s in range(1, depth):
-                self.forward(e, z_peers[s - 1], s - 1, True)
-            self.forward(e, y_peer, depth - 1, True)
-            self.forward(e, core_peer, 2 * depth - 1, True)
+            arrive(self.block(o), self.rsem.at[o])
+
+        def start_z(self):
+            self.forward(e, above, 0, True, has_above)
+            self.forward(e, below, 1, True, has_below)
+
+        def start_y(self):
+            self.forward(e, y_peer, depth + 1, True)
+            self.forward(e, core_peer, 2 * depth + 1, True)
 
         def from_z(self, s):
-            o = at(behind(s), y, c)
+            zz = nearest[s]
+            o = at(zz, y, c)
             self.wait(o)
-            self.forward(o, y_peer, depth - 1 + s)
-            self.forward(o, core_peer, 2 * depth - 1 + s)
+            self.forward(o, above, s + 1, False, jnp.logical_and(zz < z, has_above))
+            self.forward(o, below, s + 1, False, jnp.logical_and(zz > z, has_below))
+            self.forward(o, y_peer, depth + 1 + s)
+            self.forward(o, core_peer, 2 * depth + 1 + s)
             return o
 
         def from_y(self, s):
-            o = at(behind(s), 1 - y, c)
+            o = at(nearest[s], 1 - y, c)
             self.wait(o)
-            self.forward(o, core_peer, 3 * depth - 1 + s)
+            self.forward(o, core_peer, 3 * depth + 1 + s)
             return o
 
         def from_core(self, s, yy):
-            o = at(behind(s), yy, 1 - c)
+            o = at(nearest[s], yy, 1 - c)
             self.wait(o)
             return o
 
-    enc_gather = Gather(enc, enc_all, enc_recv, enc_send)
-    dec_gather = Gather(dec, dec_all, dec_recv, dec_send)
-    enc_gather.start()
+    def lat_block(o):
+        return latents.at[h, pl.ds(pl.multiple_of(o * rows, rows), rows)]
+
+    class LatentGather(Gather):
+        def start_y(self):
+            Gather.start_y(self)
+            send(lat(h, e), lat(h, e), x_lat_send.at[0], x_lat_recv.at[e], x_peer)
+
+        def from_z(self, s):
+            o = Gather.from_z(self, s)
+            send(lat(h, o), lat(h, o), x_lat_send.at[s], x_lat_recv.at[o], x_peer)
+
+        def from_y(self, s):
+            o = Gather.from_y(self, s)
+            send(lat(h, o), lat(h, o), x_lat_send.at[depth + s], x_lat_recv.at[o], x_peer)
+
+    enc_gather = Gather(enc, lambda o: enc_all.at[o], enc_recv, enc_send)
+    dec_gather = Gather(dec, lambda o: dec_all.at[o], dec_recv, dec_send)
+    pack_gather = Gather(own_pack, lambda o: pack_all.at[o], pack_recv, pack_send)
+    enc_gather.start_z()
+    enc_gather.start_y()
 
     local = [
         pltpu.make_async_copy(tokens_hbm, tokens, local_sem.at[0]),
@@ -169,75 +210,62 @@
 
     def enc_dot(o, block):
         columns = pl.ds(pl.multiple_of(o * enc_rows, enc_rows), enc_rows)
-        return jnp.dot(tokens[:, columns], block[:enc_rows], preferred_element_type=jnp.float32)
+        return jnp.dot(tokens[:, columns], block, preferred_element_type=jnp.float32)
+
+    lane = lax.broadcasted_iota(jnp.int32, (rows, 128), 1)
+    weight = jnp.zeros((rows, 128), jnp.float32)
+    for k in range(routes.shape[1]):
+        weight += jnp.where(routes[:, k : k + 1] == lane % groups, gates[:, k : k + 1], 0.0)
+    first = weight.astype(jnp.bfloat16).astype(jnp.float32)
+    second = (weight - first).astype(jnp.bfloat16).astype(jnp.float32)
+    piece = jnp.where(lane < groups, first, jnp.where(lane < 2 * groups, second, weight - first - second))
+    own_pack[...] = piece.astype(jnp.bfloat16)
 
     def take_shares(o, block):
-        pieces = half // 128
-        piece = rows // pieces
-        for q in range(pieces):
-            tile = block[enc_rows:, q * 128 : (q + 1) * 128].astype(jnp.float32)
-            lane = lax.broadcasted_iota(jnp.int32, tile.shape, 1)
-            mine = jnp.logical_and(lane % groups == e, lane < 3 * groups)
-            total = jnp.sum(jnp.where(mine, tile, 0.0), axis=1, keepdims=True)
-            start = pl.multiple_of(o * rows + q * piece, piece)
-            shares[pl.ds(start, piece), :] = jnp.broadcast_to(total, (piece, 128))
-
-    total = enc_dot(e, enc[...])
-    take_shares(e, enc[...])
-
-    def landed(o, total):
-        take_shares(o, enc_all[o])
-        return total + enc_dot(o, enc_all[o])
+        mine = jnp.logical_and(lane % groups == e, lane < 3 * groups)
+        summed = jnp.sum(jnp.where(mine, block.astype(jnp.float32), 0.0), axis=1, keepdims=True)
+        start = pl.multiple_of(o * rows, rows)
+        shares[pl.ds(start, rows), :] = jnp.broadcast_to(summed, (rows, 128))
+
+    total[...] = enc_dot(e, enc[...])
+    take_shares(e, own_pack[...])
+
+    def landed(o):
+        total[...] += enc_dot(o, enc_all[o])
 
     for s in range(1, depth + 1):
         if s < depth:
-            total = landed(enc_gather.from_z(s), total)
-        total = landed(enc_gather.from_y(s - 1), total)
-    for s in range(depth):
-        total = landed(enc_gather.from_core(s, y), total)
-    for s in range(depth):
-        total = landed(enc_gather.from_core(s, 1 - y), total)
+            o = enc_gather.from_z(s)
+            if s == depth - 1:
+                dec_gather.start_z()
+            landed(o)
+        landed(enc_gather.from_y(s - 1))
+    for yy in (y, 1 - y):
+        for s in range(depth):
+            landed(enc_gather.from_core(s, yy))
 
     def lat(hh, o):
         return latents.at[hh, pl.ds(pl.multiple_of(o * rows, rows), rows)]
 
-    def lat_forward(hh, o, peer, slot):
-        send(lat(hh, o), lat(hh, o), lat_send.at[slot], lat_recv.at[hh, o], peer)
-
-    def lat_wait(hh, o):
-        arrive(lat(hh, o), lat_recv.at[hh, o])
-
-    latents[h, pl.ds(pl.multiple_of(e * rows, rows), rows), :] = total.astype(jnp.bfloat16)
-    base_y, base_x, base_c = depth, 2 * depth, 4 * depth
-    for s in range(1, depth):
-        lat_forward(h, e, z_peers[s - 1], s - 1)
-    lat_forward(h, e, y_peer, base_y)
-    lat_forward(h, e, x_peer, base_x)
-    lat_forward(h, e, core_peer, base_c)
-
-    def lat_z(s):
-        o = at(behind(s), y, c)
-        lat_wait(h, o)
-        lat_forward(h, o, y_peer, base_y + s)
-        lat_forward(h, o, x_peer, base_x + s)
-        lat_forward(h, o, core_peer, base_c + s)
-
-    def lat_y(s):
-        o = at(behind(s), 1 - y, c)
-        lat_wait(h, o)
-        lat_forward(h, o, x_peer, base_x + depth + s)
-        lat_forward(h, o, core_peer, base_c + depth + s)
+    lat_gather = LatentGather(lat_block(e), lat_block, lat_recv, lat_send)
+    latents[h, pl.ds(pl.multiple_of(e * rows, rows), rows), :] = total[...].astype(jnp.bfloat16)
+    lat_gather.start_z()
+    lat_gather.start_y()
+    pack_gather.start_z()
+    pack_gather.start_y()
 
     def lat_x(s):
         for k, yy in enumerate((y, 1 - y)):
-            o = at(behind(s), yy, c)
-            lat_wait(1 - h, o)
-            lat_forward(1 - h, o, core_peer, base_c + (2 + k) * depth + s)
+            o = at(nearest[s], yy, c)
+            arrive(lat(1 - h, o), x_lat_recv.at[o])
+            send(lat(1 - h, o), lat(1 - h, o), core_lat_send.at[k * depth + s], core_lat_recv.at[o], core_peer)
 
     def lat_core(s):
-        for hh in (h, 1 - h):
-            for yy in (y, 1 - y):
-                lat_wait(hh, at(behind(s), yy, 1 - c))
+        for yy in (y, 1 - y):
+            o = lat_gather.from_core(s, yy)
+            arrive(lat(1 - h, o), core_lat_recv.at[o])
+            pack_gather.from_core(s, yy)
+            take_shares(o, pack_all[o])
 
     tile = 256
 
@@ -294,13 +322,22 @@
         else:
             z_out[s] = total.astype(jnp.bfloat16)
             peer = (at(behind(s), y, c), h)
-            send(z_out.at[s], z_in.at[s], z_send.at[s], z_recv.at[s], peer)
+            send(z_out.at[s], z_in.at[z], z_send.at[s], z_recv.at[z], peer)
+
+    def pack_z(s):
+        take_shares(pack_gather.from_z(s), pack_all[at(nearest[s], y, c)])
+
+    def pack_y(s):
+        take_shares(pack_gather.from_y(s), pack_all[at(nearest[s], 1 - y, c)])
 
     for s in range(1, depth + 1):
         if s < depth:
-            lat_z(s)
-        lat_y(s - 1)
-    dec_gather.start()
+            lat_gather.from_z(s)
+        lat_gather.from_y(s - 1)
+        if s < depth:
+            pack_z(s)
+        pack_y(s - 1)
+    dec_gather.start_y()
     local[1].wait()
     local[2].wait()
     own_down.wait()
@@ -311,27 +348,25 @@
         experts(s)
         if s >= 1:
             sum_cores(s - 1)
+            dec_gather.from_z(s)
         if s >= 2:
             sum_x(s - 2)
         if s >= 3:
             sum_y(s - 3)
-        if s == 0:
-            for k in range(1, depth):
-                dec_gather.from_z(k)
-        if s == 1:
-            for k in range(depth):
-                dec_gather.from_y(k)
     for s in range(depth, depth + 3):
         if s - 1 < depth:
             sum_cores(s - 1)
-        if 0 <= s - 2 < depth:
+        if s - 2 < depth:
             sum_x(s - 2)
-        if 0 <= s - 3 < depth:
+        if s - 3 < depth:
             sum_y(s - 3)
+        if s < depth + 2:
+            dec_gather.from_y(2 * (s - depth))
+            dec_gather.from_y(2 * (s - depth) + 1)
     final = keep[0, y]
     for s in range(1, depth):
-        arrive(z_in.at[s], z_recv.at[s])
-        final += z_in[s].astype(jnp.float32)
+        arrive(z_in.at[nearest[s]], z_recv.at[nearest[s]])
+        final += z_in[nearest[s]].astype(jnp.float32)
     combined[h] = final.astype(jnp.bfloat16)
     send(combined.at[h], combined.at[h], last_send.at[0], last_recv.at[0], x_peer)
     for s in range(depth):
@@ -351,28 +386,19 @@
         m += jnp.dot(combined[1], high, preferred_element_type=jnp.float32)
         out[:, columns] = m.astype(jnp.bfloat16)
 
-    for copy in waiting:
-        copy.wait_send()
+    for copy, when in waiting:
+        if when is None:
+            copy.wait_send()
+        else:
+            pl.when(when)(copy.wait_send)
 
 
 def whole_layer(tokens, enc_weight, routes, gates, gate_weight, up_weight, down_weight, dec_weight):
     groups = lax.axis_size("expert")
     depth = groups // (CORES * LINES)
     rows, width = tokens.shape
-    enc_rows, half = enc_weight.shape
+    half = enc_weight.shape[1]
     hidden = gate_weight.shape[2]
-    onehot = routes[:, :, None] == jnp.arange(groups, dtype=jnp.int32)[None, None, :]
-    rest = jnp.sum(jnp.where(onehot, gates[:, :, None], 0.0), axis=1)
-    parts = []
-    for _ in range(3):
-        piece = lax.reduce_precision(rest, 8, 7)
-        parts.append(piece.astype(jnp.bfloat16))
-        rest = rest - piece
-    packed = jnp.concatenate(parts, axis=1)
-    packed = jnp.pad(packed, ((0, 0), (0, 128 - packed.shape[1])))
-    pieces = half // 128
-    packed = packed.reshape(pieces, rows // pieces, 128).transpose(1, 0, 2).reshape(-1, half)
-    enc = jnp.concatenate([enc_weight, packed], axis=0)
     bf, f32 = jnp.bfloat16, jnp.float32
     band = LINES * CORES
     anywhere = pl.BlockSpec(memory_space=pl.ANY)
@@ -383,10 +409,13 @@
         pltpu.VMEM(gate_weight.shape[1:], bf),
         pltpu.VMEM(up_weight.shape[1:], bf),
         pltpu.VMEM((2, hidden, half), bf),
-        pltpu.VMEM((groups, *enc.shape), bf),
+        pltpu.VMEM((groups, *enc_weight.shape), bf),
         pltpu.VMEM((groups, *dec_weight.shape), bf),
         pltpu.VMEM((2, groups * rows, half), bf),
+        pltpu.VMEM((rows, 128), bf),
+        pltpu.VMEM((groups, rows, 128), bf),
         pltpu.VMEM((groups * rows, 128), f32),
+        pltpu.VMEM((rows, half), f32),
         pltpu.VMEM((band * rows, hidden), bf),
         pltpu.VMEM((depth, band, 2, rows, half), bf),
         pltpu.VMEM((depth, LINES, 2, rows, half), bf),
@@ -398,24 +427,23 @@
         pltpu.VMEM((depth, rows, half), bf),
         pltpu.VMEM((depth, rows, half), bf),
         pltpu.VMEM((2, rows, half), bf),
-        dma((groups,)), dma((4 * depth,)),
-        dma((2, groups)), dma((8 * depth,)),
-        dma((groups,)), dma((4 * depth,)),
+        *[dma((groups,)), dma((4 * depth + 1,))] * 4,
         dma((1,)), dma((1,)),
         dma((depth, LINES)), dma((depth, LINES)),
+        dma((groups,)), dma((2 * depth,)), dma((groups,)), dma((2 * depth,)),
         dma((depth,)), dma((depth,)), dma((depth,)), dma((depth,)), dma((depth,)), dma((depth,)),
         dma((1,)), dma((1,)), dma((4,)),
     ]
     return pl.pallas_call(
         layer_kernel,
         out_shape=jax.ShapeDtypeStruct((rows, dec_weight.shape[1]), bf),
-        in_specs=[anywhere, vmem, anywhere, anywhere, anywhere, vmem],
+        in_specs=[anywhere, vmem, vmem, vmem, anywhere, anywhere, anywhere, vmem],
         out_specs=vmem,
         scratch_shapes=scratch,
         compiler_params=pltpu.CompilerParams(
             collective_id=0, has_side_effects=True, vmem_limit_bytes=60 * 1024 * 1024
         ),
-    )(tokens, enc, gate_weight, up_weight, down_weight, dec_weight)
+    )(tokens, enc_weight, routes, gates, gate_weight, up_weight, down_weight, dec_weight)
 
 
 def on_device(tokens, enc_weight, routes, *rest):

time: 145 us -> 120 us (0.83); the launches traced: 145 us -> 117 us
  Pallas kernels: 140 us -> 113 us
  local copies, waits for them, and re-layouts: 2.02 us -> 4.7 us
  other arithmetic: 2.42 us -> 0 us
    pallas_call x1, Pallas kernels: 140 us -> 113 us  [whole_layer(): pl.pallas_call(layer_kernel, out_shape=jax.ShapeDtypeStruct((rows, dec_we...]
    unnamed x1 -> x3, local copies, waits for them, and re-layouts: 1.88 us -> 4.7 us
    concatenate x2 -> x0, other arithmetic: 1.69 us -> none  [the longest x1 1.68 us: whole_layer(): enc = jnp.concatenate([enc_weight, packed], axis=0)]
where the time goes in v3:
time: 120 us; the launch traced here: 117 us
  Pallas kernels  113 us (94%)
  local copies, waits for them, and re-layouts  4.7 us (4%)
    pallas_call x1, Pallas kernels, whole_layer(): pl.pallas_call(layer_kernel, out_shape=jax.ShapeDtypeStruct((rows, dec_we...  113 us
    unnamed x3, local copies, waits for them, and re-layouts  4.7 us

profile of v3, /device:TPU:0, one launch (start us, length us, event | category | flops | bytes accessed | tf_op | source)
XLA Modules:
  0.0 117.4 jit_solution(13408370296284396678)
XLA Ops:
  0.0 1.4 %copy.9.routes = s32[128,8]{1,0:T(8,128)} copy(s32[128,8]{0,1:T(8,128)} %param.10) | data formatting | bytes 8192 | tf_op args[2]
  1.4 1.4 %copy.10.gates = f32[128,8]{1,0:T(8,128)} copy(f32[128,8]{0,1:T(8,128)} %param.11) | data formatting | bytes 8192 | tf_op args[3]
  2.8 112.7 %shard_map.82 = bf16[128,2048]{1,0:T(8,128)(2,1)} custom-call(bf16[128,4096]{1,0:T(8,128)(2,1)} %tokens_hbm.1, bf16[256,512]{1,0:T(8,128)(2,1)} %enc.1, s32[128,8]{1,0:T(8,128)} %copy.9.routes, f32[128,8]{1,0:T(8,128)} %copy.10.gates, bf16[1,1024,768]{2,1,0:T(8,128)(2,1)} %gate_hbm.1, bf16[1,1024,768]{2,1,0:T(8,128)(2,1)} %up_hbm.1, ...), custom_call_target="tpu_custom_call" | custom-call | tf_op jit(solution)/shard_map/pallas_call | solution.py:437
  115.6 1.9 %copy.12 = bf16[128,2048]{1,0:T(8,128)(2,1)} copy(bf16[128,2048]{1,0:T(8,128)(2,1)} %shard_map.82) | data formatting | bytes 1048576

commit v4 on v3

--- a/solution.py
+++ b/solution.py
@@ -63,7 +63,7 @@
 
 def layer_kernel(
     tokens_hbm, enc, routes, gates, gate_hbm, up_hbm, down_hbm, dec, out,
-    tokens, gate, up, down, enc_all, dec_all, latents, own_pack, pack_all, shares, total, activation,
+    tokens, gate, up, down, enc_all, dec_all, latents, own_pack, pack_all, shares, total, mixed, activation,
     answers, core_in, x_out, x_in, keep, y_out, y_in, z_out, z_in, combined,
     enc_recv, enc_send, lat_recv, lat_send, dec_recv, dec_send,
     pack_recv, pack_send,
@@ -269,7 +269,7 @@
 
     tile = 256
 
-    def experts(s):
+    def gate_up(s, slot):
         start = pl.multiple_of(behind(s) * band, band)
 
         @pl.loop(0, gate.shape[1] // tile)
@@ -280,38 +280,50 @@
             g += jnp.dot(high, gate[half:, columns], preferred_element_type=jnp.float32)
             u = jnp.dot(low, up[:half, columns], preferred_element_type=jnp.float32)
             u += jnp.dot(high, up[half:, columns], preferred_element_type=jnp.float32)
-            activation[:, columns] = (g / (1.0 + jnp.exp(-g)) * u).astype(jnp.bfloat16)
-
+            activation[slot, :, columns] = (g / (1.0 + jnp.exp(-g)) * u).astype(jnp.bfloat16)
+
+    def down_rows(s, slot, cc):
+        blocks = [yy * CORES + cc for yy in range(LINES)]
         for hh in range(2):
             @pl.loop(0, half // tile)
             def _(n):
                 columns = pl.ds(pl.multiple_of(n * tile, tile), tile)
-                a = jnp.dot(activation[...], down[hh, :, columns], preferred_element_type=jnp.float32)
-                a = (a * shares[pl.ds(start, band), 0:1]).astype(jnp.bfloat16)
-                for b in range(LINES * CORES):
-                    answers[s, b, hh, :, columns] = a[b * rows : (b + 1) * rows]
-
+                picked = [activation[slot, pl.ds(pl.multiple_of(b * rows, rows), rows), :] for b in blocks]
+                a = jnp.dot(
+                    jnp.concatenate(picked, axis=0), down[hh, :, columns],
+                    preferred_element_type=jnp.float32,
+                )
+                for k, b in enumerate(blocks):
+                    start = pl.multiple_of(behind(s) * band + b * rows, rows)
+                    share = shares[pl.ds(start, rows), 0:1]
+                    answers[s, b, hh, :, columns] = (a[k * rows : (k + 1) * rows] * share).astype(jnp.bfloat16)
+
+    def answer_rows(s, slot):
+        down_rows(s, slot, 1 - c)
         for yy in range(LINES):
             send(
                 answers.at[s, yy * CORES + 1 - c], core_in.at[s, yy],
                 core_send.at[s, yy], core_recv.at[s, yy], core_peer,
             )
+        down_rows(s, slot, c)
 
     def sum_cores(s):
         for yy in range(LINES):
             arrive(core_in.at[s, yy], core_recv.at[s, yy])
+        for yy in (1 - y, y):
             mine = yy * CORES + c
             other = answers[s, mine, 1 - h].astype(jnp.float32)
             x_out[s, yy] = (other + core_in[s, yy, 1 - h].astype(jnp.float32)).astype(jnp.bfloat16)
-        send(x_out.at[s], x_in.at[s], x_send.at[s], x_recv.at[s], x_peer)
+            send(x_out.at[s, yy], x_in.at[s, yy], x_send.at[s, yy], x_recv.at[s, yy], x_peer)
         for yy in range(LINES):
             mine = yy * CORES + c
             keep[s, yy] = answers[s, mine, h].astype(jnp.float32) + core_in[s, yy, h].astype(jnp.float32)
 
     def sum_x(s):
-        arrive(x_in.at[s], x_recv.at[s])
+        arrive(x_in.at[s, 1 - y], x_recv.at[s, 1 - y])
         y_out[s] = (keep[s, 1 - y] + x_in[s, 1 - y].astype(jnp.float32)).astype(jnp.bfloat16)
         send(y_out.at[s], y_in.at[s], y_send.at[s], y_recv.at[s], y_peer)
+        arrive(x_in.at[s, y], x_recv.at[s, y])
         keep[s, y] = keep[s, y] + x_in[s, y].astype(jnp.float32)
 
     def sum_y(s):
@@ -342,49 +354,65 @@
     local[2].wait()
     own_down.wait()
     arrive(down.at[1 - h], down_recv.at[0])
+    last = depth - 1
+    dec_gather.from_z(1)
+    lat_x(0)
+    lat_core(0)
+    gate_up(0, 0)
+    lat_x(1)
+    lat_core(1)
+    for s in range(1, depth):
+        gate_up(s, 1)
+        if s < last:
+            lat_x(s + 1)
+        answer_rows(s, 1)
+        sum_cores(s)
+        if s < last:
+            lat_core(s + 1)
+            dec_gather.from_z(s + 1)
+        if s >= 2:
+            sum_x(s - 1)
+        if s >= 3:
+            sum_y(s - 2)
+    answer_rows(0, 0)
+    sum_cores(0)
+    if last >= 2:
+        sum_y(last - 1)
+    sum_x(last)
     for s in range(depth):
-        lat_x(s)
-        lat_core(s)
-        experts(s)
-        if s >= 1:
-            sum_cores(s - 1)
-            dec_gather.from_z(s)
-        if s >= 2:
-            sum_x(s - 2)
-        if s >= 3:
-            sum_y(s - 3)
-    for s in range(depth, depth + 3):
-        if s - 1 < depth:
-            sum_cores(s - 1)
-        if s - 2 < depth:
-            sum_x(s - 2)
-        if s - 3 < depth:
-            sum_y(s - 3)
-        if s < depth + 2:
-            dec_gather.from_y(2 * (s - depth))
-            dec_gather.from_y(2 * (s - depth) + 1)
-    final = keep[0, y]
+        dec_gather.from_y(s)
+    sum_y(last)
+    sum_x(0)
+    final = jnp.zeros((rows, half), jnp.float32)
     for s in range(1, depth):
         arrive(z_in.at[nearest[s]], z_recv.at[nearest[s]])
         final += z_in[nearest[s]].astype(jnp.float32)
-    combined[h] = final.astype(jnp.bfloat16)
-    send(combined.at[h], combined.at[h], last_send.at[0], last_recv.at[0], x_peer)
+    total[...] = final
     for s in range(depth):
         for yy in (y, 1 - y):
             dec_gather.from_core(s, yy)
     dec_all[e] = dec[...]
-    arrive(combined.at[1 - h], last_recv.at[0])
+    sum_y(0)
+    combined[h] = (total[...] + keep[0, y]).astype(jnp.bfloat16)
+    send(combined.at[h], combined.at[h], last_send.at[0], last_recv.at[0], x_peer)
 
     per = groups // 2
+
+    def product(hh, columns):
+        part = dec_all[pl.ds(pl.multiple_of(hh * per, per), per), :, columns].reshape(half, tile)
+        return jnp.dot(combined[hh], part, preferred_element_type=jnp.float32)
 
     @pl.loop(0, out.shape[1] // tile)
     def _(n):
         columns = pl.ds(pl.multiple_of(n * tile, tile), tile)
-        low = dec_all[:per, :, columns].reshape(half, tile)
-        high = dec_all[per:, :, columns].reshape(half, tile)
-        m = jnp.dot(combined[0], low, preferred_element_type=jnp.float32)
-        m += jnp.dot(combined[1], high, preferred_element_type=jnp.float32)
-        out[:, columns] = m.astype(jnp.bfloat16)
+        mixed[:, columns] = product(h, columns)
+
+    arrive(combined.at[1 - h], last_recv.at[0])
+
+    @pl.loop(0, out.shape[1] // tile)
+    def _(n):
+        columns = pl.ds(pl.multiple_of(n * tile, tile), tile)
+        out[:, columns] = (mixed[:, columns] + product(1 - h, columns)).astype(jnp.bfloat16)
 
     for copy, when in waiting:
         if when is None:
@@ -416,7 +444,8 @@
         pltpu.VMEM((groups, rows, 128), bf),
         pltpu.VMEM((groups * rows, 128), f32),
         pltpu.VMEM((rows, half), f32),
-        pltpu.VMEM((band * rows, hidden), bf),
+        pltpu.VMEM((rows, dec_weight.shape[1]), f32),
+        pltpu.VMEM((2, band * rows, hidden), bf),
         pltpu.VMEM((depth, band, 2, rows, half), bf),
         pltpu.VMEM((depth, LINES, 2, rows, half), bf),
         pltpu.VMEM((depth, LINES, rows, half), bf),
@@ -431,7 +460,7 @@
         dma((1,)), dma((1,)),
         dma((depth, LINES)), dma((depth, LINES)),
         dma((groups,)), dma((2 * depth,)), dma((groups,)), dma((2 * depth,)),
-        dma((depth,)), dma((depth,)), dma((depth,)), dma((depth,)), dma((depth,)), dma((depth,)),
+        dma((depth, LINES)), dma((depth, LINES)), dma((depth,)), dma((depth,)), dma((depth,)), dma((depth,)),
         dma((1,)), dma((1,)), dma((4,)),
     ]
     return pl.pallas_call(

time: 120 us -> 115 us (0.958); the launches traced: 117 us -> 115 us
  Pallas kernels: 113 us -> 111 us
    pallas_call x1, Pallas kernels: 113 us -> 111 us  [whole_layer(): pl.pallas_call(layer_kernel, out_shape=jax.ShapeDtypeStruct((rows, dec_we...]
where the time goes in v4:
time: 115 us
  Pallas kernels  111 us (97%)
  local copies, waits for them, and re-layouts  4.7 us (4%)
    pallas_call x1, Pallas kernels, whole_layer(): pl.pallas_call(layer_kernel, out_shape=jax.ShapeDtypeStruct((rows, dec_we...  111 us
    unnamed x3, local copies, waits for them, and re-layouts  4.7 us

profile of v4, /device:TPU:0, one launch (start us, length us, event | category | flops | bytes accessed | tf_op | source)
XLA Modules:
  0.0 115.2 jit_solution(3066664655904298224)
XLA Ops:
  0.0 1.4 %copy.9.routes = s32[128,8]{1,0:T(8,128)} copy(s32[128,8]{0,1:T(8,128)} %param.10) | data formatting | bytes 8192 | tf_op args[2]
  1.4 1.4 %copy.10.gates = f32[128,8]{1,0:T(8,128)} copy(f32[128,8]{0,1:T(8,128)} %param.11) | data formatting | bytes 8192 | tf_op args[3]
  2.8 110.5 %shard_map.82 = bf16[128,2048]{1,0:T(8,128)(2,1)} custom-call(bf16[128,4096]{1,0:T(8,128)(2,1)} %tokens_hbm.1, bf16[256,512]{1,0:T(8,128)(2,1)} %enc.1, s32[128,8]{1,0:T(8,128)} %copy.9.routes, f32[128,8]{1,0:T(8,128)} %copy.10.gates, bf16[1,1024,768]{2,1,0:T(8,128)(2,1)} %gate_hbm.1, bf16[1,1024,768]{2,1,0:T(8,128)(2,1)} %up_hbm.1, ...), custom_call_target="tpu_custom_call" | custom-call | tf_op jit(solution)/shard_map/pallas_call | solution.py:466
  113.3 1.9 %copy.12 = bf16[128,2048]{1,0:T(8,128)(2,1)} copy(bf16[128,2048]{1,0:T(8,128)(2,1)} %shard_map.82) | data formatting | bytes 1048576

commit v5 on v4

--- a/solution.py
+++ b/solution.py
@@ -240,9 +240,10 @@
                 dec_gather.start_z()
             landed(o)
         landed(enc_gather.from_y(s - 1))
-    for yy in (y, 1 - y):
-        for s in range(depth):
-            landed(enc_gather.from_core(s, yy))
+        landed(enc_gather.from_core(s - 1, y))
+        if s >= 2:
+            landed(enc_gather.from_core(s - 2, 1 - y))
+    landed(enc_gather.from_core(depth - 1, 1 - y))
 
     def lat(hh, o):
         return latents.at[hh, pl.ds(pl.multiple_of(o * rows, rows), rows)]
@@ -369,11 +370,12 @@
         sum_cores(s)
         if s < last:
             lat_core(s + 1)
-            dec_gather.from_z(s + 1)
         if s >= 2:
             sum_x(s - 1)
         if s >= 3:
             sum_y(s - 2)
+        if s < last:
+            dec_gather.from_z(s + 1)
     answer_rows(0, 0)
     sum_cores(0)
     if last >= 2:

time: 115 us -> 113 us (0.983)
  Pallas kernels: 111 us -> 108 us
    pallas_call x1, Pallas kernels: 111 us -> 108 us  [whole_layer(): pl.pallas_call(layer_kernel, out_shape=jax.ShapeDtypeStruct((rows, dec_we...]
where the time goes in v5:
time: 113 us
  Pallas kernels  108 us (96%)
  local copies, waits for them, and re-layouts  4.7 us (4%)
    pallas_call x1, Pallas kernels, whole_layer(): pl.pallas_call(layer_kernel, out_shape=jax.ShapeDtypeStruct((rows, dec_we...  108 us
    unnamed x3, local copies, waits for them, and re-layouts  4.7 us

profile of v5, /device:TPU:0, one launch (start us, length us, event | category | flops | bytes accessed | tf_op | source)
XLA Modules:
  0.0 112.7 jit_solution(8674855723731702664)
XLA Ops:
  0.0 1.4 %copy.9.routes = s32[128,8]{1,0:T(8,128)} copy(s32[128,8]{0,1:T(8,128)} %param.10) | data formatting | bytes 8192 | tf_op args[2]
  1.4 1.4 %copy.10.gates = f32[128,8]{1,0:T(8,128)} copy(f32[128,8]{0,1:T(8,128)} %param.11) | data formatting | bytes 8192 | tf_op args[3]
  2.8 108.0 %shard_map.82 = bf16[128,2048]{1,0:T(8,128)(2,1)} custom-call(bf16[128,4096]{1,0:T(8,128)(2,1)} %tokens_hbm.1, bf16[256,512]{1,0:T(8,128)(2,1)} %enc.1, s32[128,8]{1,0:T(8,128)} %copy.9.routes, f32[128,8]{1,0:T(8,128)} %copy.10.gates, bf16[1,1024,768]{2,1,0:T(8,128)(2,1)} %gate_hbm.1, bf16[1,1024,768]{2,1,0:T(8,128)(2,1)} %up_hbm.1, ...), custom_call_target="tpu_custom_call" | custom-call | tf_op jit(solution)/shard_map/pallas_call | solution.py:468
  110.9 1.9 %copy.12 = bf16[128,2048]{1,0:T(8,128)(2,1)} copy(bf16[128,2048]{1,0:T(8,128)(2,1)} %shard_map.82) | data formatting | bytes 1048576
